TPU v7x, 128 devices: a whole 4x4x4 slice. The times are simulated.
128 devices in a mesh: layer: 4 (over z_lo, core), row: 8 (over z_hi, y), col: 4 (over x).
Axes of the slice: x: 4, y: 4, z: 4 (z_hi: 2, z_lo: 2; z = z_hi * 2 + z_lo), core: 2. Of those that a mesh axis runs over, the one named last changes fastest.
Arguments:
- grad: bfloat16 [32768, 8192], P(('layer', 'row'), 'col'), parts along dimension 0, may hold values from -6 to 6
- error: bfloat16 [32768, 8192], P(('layer', 'row'), 'col'), parts along dimension 0, may hold values from -2 to 2
- left_old: bfloat16 [32768, 512], P(('layer', 'row')), parts along dimension 0, may hold values from -0.25 to 0.25
- right_old: bfloat16 [32768, 512], P(('layer', 'col')), parts along dimension 0, may hold values from -0.25 to 0.25
- first_old: float32 [2048, 512], P('layer'), parts along dimension 0, may hold values from -3 to 3
- second_old: float32 [2048, 512], P('layer'), parts along dimension 0, may hold values from 0.05 to 1
Outputs:
- error_new: bfloat16 [32768, 8192], P(('layer', 'row'), 'col'), parts along dimension 0
- first_moment: float32 [2048, 512], P('layer'), parts along dimension 0
- second_moment: float32 [2048, 512], P('layer'), parts along dimension 0
- update: float32 [2048, 512], P('layer'), parts along dimension 0
There are 4 independent parts, one for each index of `layer`. A program takes and returns all parts, laid end to end along the dimension named above; each array names one. Nothing has to cross between parts.
All inputs are finite; a program needn't handle non-finite values.
Results may differ from a plain program's by a relative error of at most 0.0075.
Values may be sent and summed in bfloat16 or wider, within the bound.
No kernel may reach another device: no remote copies, remote signals or barrier semaphores. Data moves between devices by JAX's collectives and lax.ppermute only.
A program may use at most 128 MiB of HBM per device.

v0:
```python
import jax
import jax.numpy as jnp
from jax import lax
from jax.sharding import PartitionSpec as P


def solve_rows(image, gram):
    factor = jnp.linalg.cholesky(gram)
    return jax.scipy.linalg.solve_triangular(factor, image.T, lower=True).T.astype(jnp.bfloat16)


def gram_of(image):
    return lax.dot_general(image, image, (((0,), (0,)), ((), ())), precision=lax.Precision.HIGH)


def split_pair(values):
    upper = values.astype(jnp.bfloat16)
    lower = (values - upper.astype(jnp.float32)).astype(jnp.bfloat16)
    return (upper, lower)


def per_device(grad, error, left_old, right_old, first_old, second_old):
    highest = lax.Precision.HIGHEST
    across = (((0,), (0,)), ((), ()))
    left_image = lax.psum(jnp.dot(grad, right_old, preferred_element_type=jnp.float32), "col")
    left_gram = lax.psum(gram_of(left_image), "row")
    left_basis = solve_rows(left_image, left_gram)
    right_part = lax.dot_general(grad, left_basis, across, preferred_element_type=jnp.float32)
    right_image = lax.psum(right_part, "row")
    right_gram = lax.psum(gram_of(right_image), "col")
    right_basis = solve_rows(right_image, right_gram)
    summed = grad.astype(jnp.float32) + error.astype(jnp.float32)
    accum = summed.astype(jnp.bfloat16)
    carried = jnp.dot(accum, right_basis, preferred_element_type=jnp.float32)
    carried_upper, carried_lower = split_pair(carried)
    core_part = lax.dot_general(
        left_basis, carried_upper, across, preferred_element_type=jnp.float32
    ) + lax.dot_general(left_basis, carried_lower, across, preferred_element_type=jnp.float32)
    left_count = left_basis.shape[0] // lax.axis_size("col")
    left_start = lax.axis_index("col") * left_count
    left_piece = lax.dynamic_slice_in_dim(left_basis, left_start, left_count, 0)
    left_prior = lax.dynamic_slice_in_dim(left_old, left_start, left_count, 0)
    right_count = right_basis.shape[0] // lax.axis_size("row")
    right_start = lax.axis_index("row") * right_count
    right_piece = lax.dynamic_slice_in_dim(right_basis, right_start, right_count, 0)
    right_prior = lax.dynamic_slice_in_dim(right_old, right_start, right_count, 0)
    turn_left_part = lax.dot_general(
        left_piece, left_prior, across, preferred_element_type=jnp.float32
    )
    turn_right_part = lax.dot_general(
        right_piece, right_prior, across, preferred_element_type=jnp.float32
    )
    core, turn_left, turn_right = lax.psum(
        (core_part, turn_left_part, turn_right_part), ("row", "col")
    )
    core_upper, core_lower = split_pair(core)
    lifted_full = jnp.dot(left_basis, core_upper, preferred_element_type=jnp.float32) + jnp.dot(
        left_basis, core_lower, preferred_element_type=jnp.float32
    )
    lifted = lifted_full.astype(jnp.bfloat16)
    rebuilt = lax.dot_general(
        lifted, right_basis, (((1,), (1,)), ((), ())), preferred_element_type=jnp.float32
    )
    error_new = (summed - rebuilt).astype(jnp.bfloat16)
    first_turned = jnp.dot(
        jnp.dot(turn_left, first_old, precision=highest), turn_right.T, precision=highest
    )
    excess = jnp.maximum(second_old - first_old * first_old, 0.0)
    second_turned = (
        jnp.dot(
            jnp.dot(turn_left * turn_left, excess, precision=highest),
            (turn_right * turn_right).T,
            precision=highest,
        )
        + first_turned * first_turned
    )
    first_moment = 0.9 * first_turned + 0.1 * core
    second_moment = 0.999 * second_turned + 0.001 * core * core
    update = first_moment / (jnp.sqrt(second_moment) + 0.01)
    return (error_new, first_moment, second_moment, update)


def solution(mesh):
    return jax.shard_map(
        per_device,
        mesh=mesh,
        in_specs=(
            P(("layer", "row"), "col"),
            P(("layer", "row"), "col"),
            P(("layer", "row"), None),
            P(("layer", "col"), None),
            P("layer", None),
            P("layer", None),
        ),
        out_specs=(
            P(("layer", "row"), "col"),
            P("layer", None),
            P("layer", None),
            P("layer", None),
        ),
        check_vma=False,
    )
```

profile of v0, /device:TPU:0, one launch (start us, length us, event | category | flops | bytes accessed | tf_op | source)
XLA Modules:
  0.0 1060.0 jit_solution(5173255046993698777)
XLA Ops:
  14.7 61.2 %all-reduce.8.cloned.1.call-done = f32[1024,512]{1,0:T(8,128)} async-done(((f32[1024,512]{1,0:T(8,128)}), f32[1024,512]{1,0:T(8,128)}) %all-reduce.8.cloned.1.call-update) | async-done | bytes 2097168 | tf_op jit(solution)/shard_map/psum | solution.py:25
  81.4 87.5 %all-reduce.10.cloned.1.call-done = f32[512,512]{0,1:T(8,128)} async-done(((f32[512,512]{0,1:T(8,128)}), f32[512,512]{0,1:T(8,128)}) %all-reduce.10.cloned.1.call-update) | async-done | bytes 1048592 | tf_op jit(solution)/shard_map/psum | solution.py:26
  174.0 11.7 %cholesky.286 = f32[128,128]{1,0:T(8,128)S(1)} custom-call(f32[128,128]{1,0:T(8,128)S(1)} %cholesky.426), custom_call_target="Cholesky" | custom-call | tf_op jit(solution)/shard_map/jit(cholesky)/cholesky | solution.py:8
  185.8 9.8 custom-call.33
  198.2 11.7 %cholesky.305 = f32[128,128]{1,0:T(8,128)S(1)} custom-call(f32[128,128]{1,0:T(8,128)S(1)} %cholesky.430), custom_call_target="Cholesky" | custom-call | tf_op jit(solution)/shard_map/jit(cholesky)/cholesky | solution.py:8
  209.9 10.0 custom-call.34
  221.5 11.7 %cholesky.326 = f32[128,128]{1,0:T(8,128)S(1)} custom-call(f32[128,128]{1,0:T(8,128)S(1)} %cholesky.435), custom_call_target="Cholesky" | custom-call | tf_op jit(solution)/shard_map/jit(cholesky)/cholesky | solution.py:8
  233.2 9.8 custom-call.35
  244.5 11.7 %cholesky.343 = f32[128,128]{1,0:T(8,128)S(1)} custom-call(f32[128,128]{1,0:T(8,128)S(1)} %convolution_subtract_fusion.9), custom_call_target="Cholesky" | custom-call | tf_op jit(solution)/shard_map/jit(cholesky)/cholesky | solution.py:8
  262.1 11.6 %while.2 = (s32[]{:T(128)}, f32[512,512]{1,0:T(8,128)}, s32[4,2]{0,1:T(2,128)S(1)}, f32[4,128,128]{2,1,0:T(8,128)S(1)}, s32[]{:T(128)}) while((s32[]{:T(128)}, f32[512,512]{1,0:T(8,128)}, s32[4,2]{0,1:T(2,128)S(1)}, f32[4,128,128]{2,1,0:T(8,128)S(1)}, s32[]{:T(128)}) %tuple.61), condition=%wide.while_cond, body=%wide.while_body.sunk | while | flops 2 | bytes 131189 | solution.py:9
  273.7 39.3 %custom-call.28 = f32[4,128,128]{1,2,0:T(8,128)S(1)} custom-call(f32[4,128,128]{2,1,0:T(8,128)S(1)} %get-tuple-element.12), custom_call_target="InvertDiagBlocksLowerTriangular" | custom-call | tf_op jit(solution)/shard_map/jit(_solve_triangular)/triangular_solve | solution.py:9
  330.4 108.0 %all-reduce.12.cloned.1.call-done = f32[2048,512]{0,1:T(8,128)} async-done(((f32[2048,512]{0,1:T(8,128)}), f32[2048,512]{0,1:T(8,128)}) %all-reduce.12.cloned.1.call-update) | async-done | bytes 4194320 | tf_op jit(solution)/shard_map/psum | solution.py:29
  448.8 42.1 %all-reduce.14.cloned.1.call-done = f32[512,512]{0,1:T(8,128)} async-done(((f32[512,512]{0,1:T(8,128)}), f32[512,512]{0,1:T(8,128)}) %all-reduce.14.cloned.1.call-update) | async-done | bytes 1048592 | tf_op jit(solution)/shard_map/psum | solution.py:30
  496.0 11.7 %cholesky.358 = f32[128,128]{1,0:T(8,128)S(1)} custom-call(f32[128,128]{1,0:T(8,128)S(1)} %cholesky.439), custom_call_target="Cholesky" | custom-call | tf_op jit(solution)/shard_map/jit(cholesky)/cholesky | solution.py:8
  507.9 9.8 custom-call.36
  520.9 11.7 %cholesky.377 = f32[128,128]{1,0:T(8,128)S(1)} custom-call(f32[128,128]{1,0:T(8,128)S(1)} %cholesky.443), custom_call_target="Cholesky" | custom-call | tf_op jit(solution)/shard_map/jit(cholesky)/cholesky | solution.py:8
  532.6 10.2 custom-call.37
  545.9 13.2 %cholesky.398 = f32[128,128]{1,0:T(8,128)} custom-call(f32[128,128]{1,0:T(8,128)} %cholesky.448), custom_call_target="Cholesky" | custom-call | tf_op jit(solution)/shard_map/jit(cholesky)/cholesky | solution.py:8
  560.6 11.3 %custom-call.38 = f32[1,128,128]{1,2,0:T(8,128)} custom-call(f32[1,128,128]{2,1,0:T(8,128)} %get-tuple-element.49), custom_call_target="InvertDiagBlocksLowerTriangular" | custom-call | tf_op jit(solution)/shard_map/jit(cholesky)/cholesky | solution.py:8
  574.1 11.9 %cholesky.415 = f32[128,128]{1,0:T(8,128)S(1)} custom-call(f32[128,128]{1,0:T(8,128)S(1)} %convolution_subtract_fusion.8), custom_call_target="Cholesky" | custom-call | tf_op jit(solution)/shard_map/jit(cholesky)/cholesky | solution.py:8
  592.2 11.6 %while.3 = (s32[]{:T(128)}, f32[512,512]{1,0:T(8,128)}, s32[4,2]{0,1:T(2,128)S(1)}, f32[4,128,128]{2,1,0:T(8,128)S(1)}, s32[]{:T(128)}) while((s32[]{:T(128)}, f32[512,512]{1,0:T(8,128)}, s32[4,2]{0,1:T(2,128)S(1)}, f32[4,128,128]{2,1,0:T(8,128)S(1)}, s32[]{:T(128)}) %tuple.78), condition=%wide.while_cond.1, body=%wide.while_body.1.sunk | while | flops 2 | bytes 131189 | solution.py:9
  603.8 39.3 %custom-call.29 = f32[4,128,128]{1,2,0:T(8,128)S(1)} custom-call(f32[4,128,128]{2,1,0:T(8,128)S(1)} %get-tuple-element.20), custom_call_target="InvertDiagBlocksLowerTriangular" | custom-call | tf_op jit(solution)/shard_map/jit(_solve_triangular)/triangular_solve | solution.py:9
  665.1 362.9 %all-reduce.16.cloned.1.call-done = (f32[512,512]{1,0:T(8,128)}, f32[512,512]{1,0:T(8,128)}, f32[512,512]{1,0:T(8,128)}) async-done(((f32[512,512]{1,0:T(8,128)}, f32[512,512]{1,0:T(8,128)}, f32[512,512]{1,0:T(8,128)}), (f32[512,512]{1,0:T(8,128)}, f32[512,512]{1,0:T(8,128)}, f32[512,512]{1,0:T(8,128)})) %all-reduce.16.cloned.1.call-update) | async-done | bytes 3145744 | tf_op jit(solution)/shard_map/psum | solution.py:53
  1031.6 10.4 subtract_convert_fusion
  (161 shorter events, 133.2 us)
Async XLA Ops:
  7.2 68.7 %all-reduce.8.cloned.1.call-start = ((), (), s32[]{:S(2)}) async-start(), calls=%async_computation | async-start | bytes 4194304 | tf_op jit(solution)/shard_map/psum | solution.py:25
  14.6 154.3 %all-reduce.10.cloned.1.call-start = ((), (), s32[]{:S(2)}) async-start(), calls=%async_computation.1 | async-start | bytes 2097152 | tf_op jit(solution)/shard_map/psum | solution.py:26
  80.9 357.4 %all-reduce.12.cloned.1.call-start = ((), (), s32[]{:S(2)}) async-start(), calls=%async_computation.2 | async-start | bytes 8388608 | tf_op jit(solution)/shard_map/psum | solution.py:29
  168.9 2.6 copy-start.5
  313.0 4.7 copy-start.2
  314.9 131.6 %copy-start.16 = (bf16[128,1024]{1,0:T(8,128)(2,1)}, bf16[128,1024]{1,0:T(8,128)(2,1)S(1)}, u32[]{:S(2)}) copy-start(bf16[128,1024]{1,0:T(8,128)(2,1)S(1)} %get-tuple-element.72) | copy-start | bytes 786436
  317.7 128.8 %copy-start.18 = (bf16[128,1024]{1,0:T(8,128)(2,1)}, bf16[128,1024]{1,0:T(8,128)(2,1)S(1)}, u32[]{:S(2)}) copy-start(bf16[128,1024]{1,0:T(8,128)(2,1)S(1)} %get-tuple-element.70) | copy-start | bytes 786436
  320.5 5.3 copy-start.24
  321.2 125.3 %copy-start.20 = (bf16[128,1024]{1,0:T(8,128)(2,1)}, bf16[128,1024]{1,0:T(8,128)(2,1)S(1)}, u32[]{:S(2)}) copy-start(bf16[128,1024]{1,0:T(8,128)(2,1)S(1)} %get-tuple-element.68) | copy-start | bytes 786436
  330.3 160.6 %all-reduce.14.cloned.1.call-start = ((), (), s32[]{:S(2)}) async-start(), calls=%async_computation.3 | async-start | bytes 2097152 | tf_op jit(solution)/shard_map/psum | solution.py:30
  446.2 581.8 %all-reduce.16.cloned.1.call-start = ((), (), s32[]{:S(2)}) async-start(), calls=%async_computation.4 | async-start | bytes 6291456 | tf_op jit(solution)/shard_map/psum | solution.py:53
  490.9 2.6 copy-start.4
  645.4 11.5 %copy-start.11 = (bf16[128,2048]{1,0:T(8,128)(2,1)}, bf16[128,2048]{1,0:T(8,128)(2,1)S(1)}, u32[]{:S(2)}) copy-start(bf16[128,2048]{1,0:T(8,128)(2,1)S(1)} %get-tuple-element.80) | copy-start | bytes 1572868
  645.4 3.6 copy-start.1
  648.9 7.9 copy-start.12
  652.3 4.6 copy-start.13
  652.3 5.1 copy-start.25
  656.6 2.4 copy-start.23
  659.0 2.4 copy-start.17
  659.0 2.4 copy-start.19
  659.0 2.4 copy-start.21
  1031.6 10.5 copy-start.6
  1042.0 3.2 copy-start.7
  1042.0 3.2 copy-start.15
  (7 other events, 8.9 us)
Sparse Core Ops, SparseCore 0:
  14.7 61.0 all-reduce.7
  81.0 87.8 all-reduce.9
  330.4 107.8 all-reduce.11
  446.4 44.5 all-reduce.13
  665.3 362.7 all-reduce.15
where the time goes:
time: 1060 us
  waiting for transfers between devices  662 us (62%)
  other arithmetic  247 us (23%)
  matrix products  95.3 us (9%)
  local copies, waits for them, and re-layouts  35.5 us (3%)
  between operations  19.7 us (2%)
    psum x1, waiting for transfers between devices, per_device(): lax.psum((core_part, turn_left_part, turn_right_part), ('row', 'col'))  363 us
    another operation x29, other arithmetic, solve_rows(): factor = jnp.linalg.cholesky(gram)  162 us
    psum x1, waiting for transfers between devices, per_device(): right_image = lax.psum(right_part, 'row')  108 us
    psum x1, waiting for transfers between devices, per_device(): left_gram = lax.psum(gram_of(left_image), 'row')  87.5 us
    another operation x7, other arithmetic, solve_rows(): jax.scipy.linalg.solve_triangular(factor, image.T, lower=True)  81.5 us
    psum x1, waiting for transfers between devices, per_device(): lax.psum(jnp.dot(grad, right_old, preferred_element_type=jnp.float32), 'c...  61.2 us
    psum x1, waiting for transfers between devices, per_device(): right_gram = lax.psum(gram_of(right_image), 'col')  42.1 us
    another operation x14, matrix products, solve_rows(): jax.scipy.linalg.solve_triangular(factor, image.T, lower=True)  26.1 us
  transfers between devices with their start and end apart: 5, of which 5 were waited for; matrix products, arithmetic and copies ran while one was open for 0% of the time, Pallas kernels for 0%

commit v1 on v0

--- a/solution.py
+++ b/solution.py
@@ -2,6 +2,11 @@
 import jax.numpy as jnp
 from jax import lax
 from jax.sharding import PartitionSpec as P
+
+
+def by_each_axis(value, one, other):
+    partial = lax.psum(value, one)
+    return lax.psum(partial, other)
 
 
 def solve_rows(image, gram):
@@ -50,8 +55,8 @@
     turn_right_part = lax.dot_general(
         right_piece, right_prior, across, preferred_element_type=jnp.float32
     )
-    core, turn_left, turn_right = lax.psum(
-        (core_part, turn_left_part, turn_right_part), ("row", "col")
+    core, turn_left, turn_right = by_each_axis(
+        (core_part, turn_left_part, turn_right_part), "row", "col"
     )
     core_upper, core_lower = split_pair(core)
     lifted_full = jnp.dot(left_basis, core_upper, preferred_element_type=jnp.float32) + jnp.dot(

time: 1060 us -> 881 us (0.83)
  waiting for transfers between devices: 662 us -> 476 us
    psum x1 -> x2, waiting for transfers between devices: 363 us -> 177 us  [the longest x1 101 us: by_each_axis(): partial = lax.psum(value, one)]
  transfers between devices with their start and end apart: 5 -> 6, of which waited for: 5 -> 6; matrix products, arithmetic and copies ran while one was open for 0% -> 0% of each run, Pallas kernels for 0% -> 0%
where the time goes in v1:
time: 881 us; the launch traced here: 875 us
  waiting for transfers between devices  476 us (54%)
  other arithmetic  247 us (28%)
  matrix products  95.2 us (11%)
  local copies, waits for them, and re-layouts  35.5 us (4%)
  between operations  20.2 us (2%)
    another operation x29, other arithmetic, solve_rows(): factor = jnp.linalg.cholesky(gram)  162 us
    psum x1, waiting for transfers between devices, per_device(): right_image = lax.psum(right_part, 'row')  108 us
    psum x1, waiting for transfers between devices, by_each_axis(): partial = lax.psum(value, one)  101 us
    psum x1, waiting for transfers between devices, per_device(): left_gram = lax.psum(gram_of(left_image), 'row')  87.5 us
    another operation x7, other arithmetic, solve_rows(): jax.scipy.linalg.solve_triangular(factor, image.T, lower=True)  81.5 us
    psum x1, waiting for transfers between devices, by_each_axis(): return lax.psum(partial, other)  76.6 us
    psum x1, waiting for transfers between devices, per_device(): lax.psum(jnp.dot(grad, right_old, preferred_element_type=jnp.float32), 'c...  61.2 us
    psum x1, waiting for transfers between devices, per_device(): right_gram = lax.psum(gram_of(right_image), 'col')  42.1 us
  transfers between devices with their start and end apart: 6, of which 6 were waited for; matrix products, arithmetic and copies ran while one was open for 0% of the time, Pallas kernels for 0%

profile of v1, /device:TPU:0, one launch (start us, length us, event | category | flops | bytes accessed | tf_op | source)
XLA Modules:
  0.0 875.4 jit_solution(5211227880351939616)
XLA Ops:
  14.7 61.2 %all-reduce.10.cloned.1.call-done = f32[1024,512]{1,0:T(8,128)} async-done(((f32[1024,512]{1,0:T(8,128)}), f32[1024,512]{1,0:T(8,128)}) %all-reduce.10.cloned.1.call-update) | async-done | bytes 2097168 | tf_op jit(solution)/shard_map/psum | solution.py:30
  81.4 87.5 %all-reduce.12.cloned.1.call-done = f32[512,512]{0,1:T(8,128)} async-done(((f32[512,512]{0,1:T(8,128)}), f32[512,512]{0,1:T(8,128)}) %all-reduce.12.cloned.1.call-update) | async-done | bytes 1048592 | tf_op jit(solution)/shard_map/psum | solution.py:31
  174.0 11.7 %cholesky.286 = f32[128,128]{1,0:T(8,128)S(1)} custom-call(f32[128,128]{1,0:T(8,128)S(1)} %cholesky.426), custom_call_target="Cholesky" | custom-call | tf_op jit(solution)/shard_map/jit(cholesky)/cholesky | solution.py:13
  185.8 9.8 %custom-call.33 = f32[1,128,128]{1,2,0:T(8,128)S(1)} custom-call(f32[1,128,128]{2,1,0:T(8,128)S(1)} %get-tuple-element.68), custom_call_target="InvertDiagBlocksLowerTriangular" | custom-call | tf_op jit(solution)/shard_map/jit(cholesky)/cholesky | solution.py:13
  198.2 11.7 %cholesky.305 = f32[128,128]{1,0:T(8,128)S(1)} custom-call(f32[128,128]{1,0:T(8,128)S(1)} %cholesky.430), custom_call_target="Cholesky" | custom-call | tf_op jit(solution)/shard_map/jit(cholesky)/cholesky | solution.py:13
  209.9 10.0 %custom-call.34 = f32[1,128,128]{1,2,0:T(8,128)S(1)} custom-call(f32[1,128,128]{2,1,0:T(8,128)S(1)} %get-tuple-element.65), custom_call_target="InvertDiagBlocksLowerTriangular" | custom-call | tf_op jit(solution)/shard_map/jit(cholesky)/cholesky | solution.py:13
  221.5 11.7 %cholesky.326 = f32[128,128]{1,0:T(8,128)S(1)} custom-call(f32[128,128]{1,0:T(8,128)S(1)} %cholesky.435), custom_call_target="Cholesky" | custom-call | tf_op jit(solution)/shard_map/jit(cholesky)/cholesky | solution.py:13
  233.2 9.8 %custom-call.35 = f32[1,128,128]{1,2,0:T(8,128)S(1)} custom-call(f32[1,128,128]{2,1,0:T(8,128)S(1)} %get-tuple-element.62), custom_call_target="InvertDiagBlocksLowerTriangular" | custom-call | tf_op jit(solution)/shard_map/jit(cholesky)/cholesky | solution.py:13
  244.5 11.7 %cholesky.343 = f32[128,128]{1,0:T(8,128)S(1)} custom-call(f32[128,128]{1,0:T(8,128)S(1)} %convolution_subtract_fusion.9), custom_call_target="Cholesky" | custom-call | tf_op jit(solution)/shard_map/jit(cholesky)/cholesky | solution.py:13
  262.2 11.6 %while.2 = (s32[]{:T(128)}, f32[512,512]{1,0:T(8,128)}, s32[4,2]{0,1:T(2,128)S(1)}, f32[4,128,128]{2,1,0:T(8,128)S(1)}, s32[]{:T(128)}) while((s32[]{:T(128)}, f32[512,512]{1,0:T(8,128)}, s32[4,2]{0,1:T(2,128)S(1)}, f32[4,128,128]{2,1,0:T(8,128)S(1)}, s32[]{:T(128)}) %tuple.61), condition=%wide.while_cond, body=%wide.while_body.sunk | while | flops 2 | bytes 131189 | solution.py:14
  273.8 39.3 %custom-call.28 = f32[4,128,128]{1,2,0:T(8,128)S(1)} custom-call(f32[4,128,128]{2,1,0:T(8,128)S(1)} %get-tuple-element.12), custom_call_target="InvertDiagBlocksLowerTriangular" | custom-call | tf_op jit(solution)/shard_map/jit(_solve_triangular)/triangular_solve | solution.py:14
  330.5 108.0 %all-reduce.14.cloned.1.call-done = f32[2048,512]{0,1:T(8,128)} async-done(((f32[2048,512]{0,1:T(8,128)}), f32[2048,512]{0,1:T(8,128)}) %all-reduce.14.cloned.1.call-update) | async-done | bytes 4194320 | tf_op jit(solution)/shard_map/psum | solution.py:34
  449.0 42.1 %all-reduce.16.cloned.1.call-done = f32[512,512]{0,1:T(8,128)} async-done(((f32[512,512]{0,1:T(8,128)}), f32[512,512]{0,1:T(8,128)}) %all-reduce.16.cloned.1.call-update) | async-done | bytes 1048592 | tf_op jit(solution)/shard_map/psum | solution.py:35
  496.1 11.7 %cholesky.358 = f32[128,128]{1,0:T(8,128)S(1)} custom-call(f32[128,128]{1,0:T(8,128)S(1)} %cholesky.439), custom_call_target="Cholesky" | custom-call | tf_op jit(solution)/shard_map/jit(cholesky)/cholesky | solution.py:13
  521.0 11.7 %cholesky.377 = f32[128,128]{1,0:T(8,128)S(1)} custom-call(f32[128,128]{1,0:T(8,128)S(1)} %cholesky.443), custom_call_target="Cholesky" | custom-call | tf_op jit(solution)/shard_map/jit(cholesky)/cholesky | solution.py:13
  532.8 10.2 %custom-call.37 = f32[1,128,128]{1,2,0:T(8,128)S(1)} custom-call(f32[1,128,128]{2,1,0:T(8,128)S(1)} %get-tuple-element.55), custom_call_target="InvertDiagBlocksLowerTriangular" | custom-call | tf_op jit(solution)/shard_map/jit(cholesky)/cholesky | solution.py:13
  546.1 13.2 %cholesky.398 = f32[128,128]{1,0:T(8,128)} custom-call(f32[128,128]{1,0:T(8,128)} %cholesky.448), custom_call_target="Cholesky" | custom-call | tf_op jit(solution)/shard_map/jit(cholesky)/cholesky | solution.py:13
  560.8 11.3 %custom-call.38 = f32[1,128,128]{1,2,0:T(8,128)} custom-call(f32[1,128,128]{2,1,0:T(8,128)} %get-tuple-element.52), custom_call_target="InvertDiagBlocksLowerTriangular" | custom-call | tf_op jit(solution)/shard_map/jit(cholesky)/cholesky | solution.py:13
  574.3 11.9 %cholesky.415 = f32[128,128]{1,0:T(8,128)S(1)} custom-call(f32[128,128]{1,0:T(8,128)S(1)} %convolution_subtract_fusion.8), custom_call_target="Cholesky" | custom-call | tf_op jit(solution)/shard_map/jit(cholesky)/cholesky | solution.py:13
  592.6 11.6 %while.3 = (s32[]{:T(128)}, f32[512,512]{1,0:T(8,128)}, s32[4,2]{0,1:T(2,128)S(1)}, f32[4,128,128]{2,1,0:T(8,128)S(1)}, s32[]{:T(128)}) while((s32[]{:T(128)}, f32[512,512]{1,0:T(8,128)}, s32[4,2]{0,1:T(2,128)S(1)}, f32[4,128,128]{2,1,0:T(8,128)S(1)}, s32[]{:T(128)}) %tuple.81), condition=%wide.while_cond.1, body=%wide.while_body.1.sunk | while | flops 2 | bytes 131189 | solution.py:14
  604.1 39.3 %custom-call.29 = f32[4,128,128]{1,2,0:T(8,128)S(1)} custom-call(f32[4,128,128]{2,1,0:T(8,128)S(1)} %get-tuple-element.20), custom_call_target="InvertDiagBlocksLowerTriangular" | custom-call | tf_op jit(solution)/shard_map/jit(_solve_triangular)/triangular_solve | solution.py:14
  665.7 100.8 %all-reduce.18.cloned.1.call-done = (f32[512,512]{1,0:T(8,128)}, f32[512,512]{1,0:T(8,128)}, f32[512,512]{1,0:T(8,128)}) async-done(((f32[512,512]{1,0:T(8,128)}, f32[512,512]{1,0:T(8,128)}, f32[512,512]{1,0:T(8,128)}), (f32[512,512]{1,0:T(8,128)}, f32[512,512]{1,0:T(8,128)}, f32[512,512]{1,0:T(8,128)})) %all-reduce.18.cloned.1.call-update) | async-done | bytes 3145744 | tf_op jit(solution)/shard_map/psum | solution.py:8
  766.6 76.6 %all-reduce.20.cloned.1.call-done = (f32[512,512]{1,0:T(8,128)}, f32[512,512]{1,0:T(8,128)}, f32[512,512]{1,0:T(8,128)}) async-done(((f32[512,512]{1,0:T(8,128)}, f32[512,512]{1,0:T(8,128)}, f32[512,512]{1,0:T(8,128)}), (f32[512,512]{1,0:T(8,128)}, f32[512,512]{1,0:T(8,128)}, f32[512,512]{1,0:T(8,128)})) %all-reduce.20.cloned.1.call-update) | async-done | bytes 3145744 | tf_op jit(solution)/shard_map/psum | solution.py:9
  846.5 10.6 %subtract_convert_fusion = bf16[1024,2048]{1,0:T(8,128)(2,1)} fusion(bf16[1024,2048]{1,0:T(8,128)(2,1)} %param.8, bf16[1024,2048]{1,0:T(8,128)(2,1)} %param.7, f32[1024,512]{1,0:T(8,128)} %fusion.55, f32[512,512]{1,0:T(8,128)} %get-tuple-element.40, bf16[128,2048]{1,0:T(8,128)(2,1)} %copy-done.10, bf16[128,2048]{1,0:T(8,128)(2,1)} %copy-done.13, ...), kind=kOutput, calls=%fused_computation.4 | convolution fusion | flops 2709520384 | bytes 18874368 | tf_op jit(solution)/shard_map/dot_general | solution.py:66
  (164 shorter events, 143.2 us)
Async XLA Ops:
  7.2 68.7 %all-reduce.10.cloned.1.call-start = ((), (), s32[]{:S(2)}) async-start(), calls=%async_computation | async-start | bytes 4194304 | tf_op jit(solution)/shard_map/psum | solution.py:30
  14.6 154.3 %all-reduce.12.cloned.1.call-start = ((), (), s32[]{:S(2)}) async-start(), calls=%async_computation.1 | async-start | bytes 2097152 | tf_op jit(solution)/shard_map/psum | solution.py:31
  80.9 357.6 %all-reduce.14.cloned.1.call-start = ((), (), s32[]{:S(2)}) async-start(), calls=%async_computation.2 | async-start | bytes 8388608 | tf_op jit(solution)/shard_map/psum | solution.py:34
  168.9 2.6 copy-start.5
  313.1 4.7 copy-start.2
  315.0 131.7 %copy-start.16 = (bf16[128,1024]{1,0:T(8,128)(2,1)}, bf16[128,1024]{1,0:T(8,128)(2,1)S(1)}, u32[]{:S(2)}) copy-start(bf16[128,1024]{1,0:T(8,128)(2,1)S(1)} %get-tuple-element.75) | copy-start | bytes 786436
  317.8 128.8 %copy-start.18 = (bf16[128,1024]{1,0:T(8,128)(2,1)}, bf16[128,1024]{1,0:T(8,128)(2,1)S(1)}, u32[]{:S(2)}) copy-start(bf16[128,1024]{1,0:T(8,128)(2,1)S(1)} %get-tuple-element.73) | copy-start | bytes 786436
  320.7 5.3 copy-start.24
  321.3 125.4 %copy-start.20 = (bf16[128,1024]{1,0:T(8,128)(2,1)}, bf16[128,1024]{1,0:T(8,128)(2,1)S(1)}, u32[]{:S(2)}) copy-start(bf16[128,1024]{1,0:T(8,128)(2,1)S(1)} %get-tuple-element.71) | copy-start | bytes 786436
  330.4 160.7 %all-reduce.16.cloned.1.call-start = ((), (), s32[]{:S(2)}) async-start(), calls=%async_computation.3 | async-start | bytes 2097152 | tf_op jit(solution)/shard_map/psum | solution.py:35
  446.4 320.2 %all-reduce.18.cloned.1.call-start = ((), (), s32[]{:S(2)}) async-start(), calls=%async_computation.4 | async-start | bytes 6291456 | tf_op jit(solution)/shard_map/psum | solution.py:8
  491.1 2.6 copy-start.4
  645.7 11.5 %copy-start.11 = (bf16[128,2048]{1,0:T(8,128)(2,1)}, bf16[128,2048]{1,0:T(8,128)(2,1)S(1)}, u32[]{:S(2)}) copy-start(bf16[128,2048]{1,0:T(8,128)(2,1)S(1)} %get-tuple-element.83) | copy-start | bytes 1572868
  645.7 3.6 copy-start.1
  649.3 7.9 copy-start.12
  652.7 4.6 copy-start.13
  652.7 5.0 copy-start.25
  659.3 2.4 copy-start.17
  659.4 2.4 copy-start.19
  659.4 2.4 copy-start.21
  665.5 177.7 %all-reduce.20.cloned.1.call-start = ((), (), s32[]{:S(2)}) async-start(), calls=%async_computation.5 | async-start | bytes 6291456 | tf_op jit(solution)/shard_map/psum | solution.py:9
  846.5 10.6 %copy-start.6 = (f32[512,512]{1,0:T(8,128)S(1)}, f32[512,512]{1,0:T(8,128)}, u32[]{:S(2)}) copy-start(f32[512,512]{1,0:T(8,128)} %param.11) | copy-start | bytes 3145732
  857.1 3.2 copy-start.7
  857.1 3.2 copy-start.15
  (8 other events, 11.3 us)
Sparse Core Ops, SparseCore 0:
  14.7 61.0 all-reduce.9
  81.0 87.8 all-reduce.11
  330.5 107.9 all-reduce.13
  446.5 44.5 all-reduce.15
  665.6 100.9 all-reduce.17
  769.0 74.2 all-reduce.19
